TPU v7x, 32 devices: a whole 2x2x4 slice. The times are simulated.
32 devices in a mesh: row: 4 (over z), col: 8 (over y, x, core).
Axes of the slice: x: 2, y: 2, z: 4, core: 2. Of those that a mesh axis runs over, the one named last changes fastest.
Arguments:
- tokens: bfloat16 [512, 8192], P('col', 'row'), may hold values from -6 to 6
- w_gate: bfloat16 [8192, 16384], P('row', 'col'), may hold values from -0.09375 to 0.09375
- w_up: bfloat16 [8192, 16384], P('row', 'col'), may hold values from -0.09375 to 0.09375
- w_down: bfloat16 [16384, 8192], P('col', 'row'), may hold values from -0.0625 to 0.0625
- mask_in: int32 [64, 32], P('col', 'row'), may hold values 0 or 1
- mask_out: int32 [64, 32], P('col', 'row'), may hold values 0 or 1
- out_grad: bfloat16 [512, 8192], P('col', 'row'), may hold values from -6 to 6
Outputs:
- output: bfloat16 [512, 8192], P('col', 'row')
- tokens_grad: bfloat16 [512, 8192], P('col', 'row')
- gate_wgrad: bfloat16 [8192, 16384], P('row', 'col')
- up_wgrad: bfloat16 [8192, 16384], P('row', 'col')
- down_wgrad: bfloat16 [16384, 8192], P('col', 'row')
All inputs are finite; a program needn't handle non-finite values. No bound on the sum of `mask_in` or of `mask_out` on one device may be relied on, other than what follows from the above.
Results may differ from a plain program's by a relative error of at most 0.0049.
Values may be sent and summed in bfloat16 or wider, within the bound.
A program may use at most 128 MiB of HBM per device.

v0:
```python
import jax
import jax.numpy as jnp
from jax import lax
from jax.sharding import PartitionSpec as P

BLOCK = 256


def spread(mask_tile):
    return jnp.repeat(jnp.repeat(mask_tile.T, BLOCK, axis=0), BLOCK, axis=1)


def transposed_right(left, right):
    return lax.dot_general(
        left, right, (((1,), (1,)), ((), ())), preferred_element_type=jnp.float32
    )


def transposed_left(left, right):
    return lax.dot_general(
        left, right, (((0,), (0,)), ((), ())), preferred_element_type=jnp.float32
    )


def local(tokens, w_gate, w_up, w_down, mask_in, mask_out, out_grad):
    keep_in = spread(mask_in).astype(jnp.bfloat16)
    keep_out = spread(mask_out).T.astype(jnp.bfloat16)
    gate_masked = w_gate * keep_in
    up_masked = w_up * keep_in
    down_masked = w_down * keep_out
    hidden_width = w_gate.shape[1]
    x_panel = lax.all_gather(tokens, "col", axis=0, tiled=True)
    row_block = x_panel
    gate_part = jnp.dot(row_block, gate_masked, preferred_element_type=jnp.float32)
    up_part = jnp.dot(row_block, up_masked, preferred_element_type=jnp.float32)
    joined = lax.psum_scatter(
        jnp.concatenate([gate_part, up_part], axis=1), "row", scatter_dimension=0, tiled=True
    )
    gate = joined[:, :hidden_width]
    up = joined[:, hidden_width:]
    sigmoid_gate = jax.nn.sigmoid(gate)
    hidden_share = (gate * sigmoid_gate * up).astype(jnp.bfloat16)
    hidden_full = lax.all_gather(hidden_share, "row", axis=0, tiled=True)
    row_block = hidden_full
    output = lax.psum_scatter(
        jnp.dot(row_block, down_masked, preferred_element_type=jnp.float32),
        "col",
        scatter_dimension=0,
        tiled=True,
    ).astype(jnp.bfloat16)
    dy_panel = lax.all_gather(out_grad, "col", axis=0, tiled=True)
    down_wgrad = (transposed_left(hidden_full, dy_panel) * keep_out.astype(jnp.float32)).astype(
        jnp.bfloat16
    )
    row_block = dy_panel
    hidden_grad = lax.psum_scatter(
        transposed_right(row_block, down_masked), "row", scatter_dimension=0, tiled=True
    )
    up_grad = (hidden_grad * gate * sigmoid_gate).astype(jnp.bfloat16)
    gate_grad = (hidden_grad * up * sigmoid_gate * (1.0 + gate * (1.0 - sigmoid_gate))).astype(
        jnp.bfloat16
    )
    gate_full, up_full = (
        lax.all_gather(gate_grad, "row", axis=0, tiled=True),
        lax.all_gather(up_grad, "row", axis=0, tiled=True),
    )
    keep_wide = keep_in.astype(jnp.float32)
    gate_wgrad = (transposed_left(x_panel, gate_full) * keep_wide).astype(jnp.bfloat16)
    up_wgrad = (transposed_left(x_panel, up_full) * keep_wide).astype(jnp.bfloat16)
    tokens_grad = lax.psum_scatter(
        transposed_right(gate_full, gate_masked) + transposed_right(up_full, up_masked),
        "col",
        scatter_dimension=0,
        tiled=True,
    ).astype(jnp.bfloat16)
    return (output, tokens_grad, gate_wgrad, up_wgrad, down_wgrad)


def solution(mesh):
    placed = (
        P("col", "row"),
        P("row", "col"),
        P("row", "col"),
        P("col", "row"),
        P("col", "row"),
        P("col", "row"),
        P("col", "row"),
    )
    return jax.shard_map(
        local,
        mesh=mesh,
        in_specs=placed,
        out_specs=(
            P("col", "row"),
            P("col", "row"),
            P("row", "col"),
            P("row", "col"),
            P("col", "row"),
        ),
        check_vma=False,
    )
```

profile of v0, /device:TPU:0, one launch (start us, length us, event | category | flops | bytes accessed | tf_op | source)
XLA Modules:
  0.0 554.7 jit_solution(6437327898248120053)
XLA Ops:
  9.6 7.3 %bitcast_multiply_fusion.2 = bf16[2048,2048]{1,0:T(8,128)(2,1)} fusion(bf16[2048,2048]{1,0:T(8,128)(2,1)} %param.10, bf16[2048,8]{0,1:T(8,128)(2,1)S(1)} %bitcast.48), kind=kLoop, calls=%fused_computation.7 | loop fusion | flops 4194304 | bytes 16809984 | tf_op jit(solution)/shard_map/mul | solution.py:30
  16.9 23.5 %all-gather.10.cloned.1.call-done = bf16[512,2048]{1,0:T(8,128)(2,1)} async-done(((bf16[64,2048]{1,0:T(8,128)(2,1)}), bf16[512,2048]{1,0:T(8,128)(2,1)}) %all-gather.10.cloned.1.call-update) | async-done | bytes 2097168 | tf_op jit(solution)/shard_map/all_gather | solution.py:51
  40.4 10.5 %convolution_bitcast_fusion = f32[512,2048]{0,1:T(8,128)} fusion(bf16[2048,2048]{1,0:T(8,128)(2,1)} %bitcast_multiply_fusion.2, bf16[512,2048]{1,0:T(8,128)(2,1)} %all-gather.10.cloned.1.call-done), kind=kOutput, calls=%fused_computation.9 | convolution fusion | flops 4294967296 | bytes 14680064 | tf_op jit(solution)/shard_map/dot_general | solution.py:14
  51.7 12.2 %copy.13 = bf16[2048,2048]{0,1:T(8,128)(2,1)} copy(bf16[2048,2048]{1,0:T(8,128)(2,1)} %param.8) | data formatting | bytes 16777216 | tf_op args[1]
  63.9 12.2 %copy.14 = bf16[2048,2048]{0,1:T(8,128)(2,1)} copy(bf16[2048,2048]{1,0:T(8,128)(2,1)} %param.9) | data formatting | bytes 16777216 | tf_op args[2]
  76.2 13.7 %bitcast_multiply_fusion.1 = (bf16[2048,2048]{0,1:T(8,128)(2,1)}, bf16[2048,2048]{0,1:T(8,128)(2,1)}) fusion(bf16[2048,2048]{0,1:T(8,128)(2,1)} %copy.13, bf16[2048,8]{0,1:T(8,128)(2,1)S(1)} %bitcast.50, bf16[2048,2048]{0,1:T(8,128)(2,1)} %copy.14), kind=kLoop, calls=%fused_computation.3 | loop fusion | flops 8388608 | bytes 33587200 | tf_op jit(solution)/shard_map/mul | solution.py:28
  89.9 7.8 %convolution_bitcast_fusion.1 = f32[512,2048]{0,1:T(8,128)S(1)} fusion(bf16[2048,2048]{0,1:T(8,128)(2,1)} %get-tuple-element.14, bf16[512,2048]{1,0:T(8,128)(2,1)} %all-gather.6.cloned.1.call-done), kind=kOutput, calls=%fused_computation.10 | convolution fusion | flops 4294967296 | bytes 14680064 | tf_op jit(solution)/shard_map/dot_general | solution.py:35
  97.7 4.8 convolution_bitcast_fusion.2
  102.5 4.2 pad_maximum_fusion
  106.8 42.4 %reduce-scatter.9.cloned.1.call-done = f32[128,2048]{0,1:T(8,128)} async-done(((f32[512,2048]{0,1:T(8,128)}), f32[128,2048]{0,1:T(8,128)}) %reduce-scatter.9.cloned.1.call-update) | async-done | bytes 1048592 | tf_op jit(solution)/shard_map/reduce_scatter | solution.py:56
  149.2 147.4 %reduce-scatter.5.cloned.1.call-done = f32[128,4096]{0,1:T(8,128)} async-done(((f32[512,4096]{0,1:T(8,128)}), f32[128,4096]{0,1:T(8,128)}) %reduce-scatter.5.cloned.1.call-update) | async-done | bytes 2097168 | tf_op jit(solution)/shard_map/reduce_scatter | solution.py:36
  296.6 3.5 multiply_convert_fusion.1
  301.7 45.4 %all-gather.12.cloned.1.call-done = bf16[512,2048]{0,1:T(8,128)(2,1)} async-done(((bf16[128,2048]{0,1:T(8,128)(2,1)}), bf16[512,2048]{0,1:T(8,128)(2,1)}) %all-gather.12.cloned.1.call-update) | async-done | bytes 2097168 | tf_op jit(solution)/shard_map/all_gather | solution.py:64
  347.1 10.6 %fusion.3 = f32[512,2048]{1,0:T(8,128)} fusion(bf16[512,2048]{0,1:T(8,128)(2,1)} %all-gather.12.cloned.1.call-done, bf16[2048,2048]{0,1:T(8,128)(2,1)} %get-tuple-element.13), kind=kOutput, calls=%fused_computation.20 | convolution fusion | flops 4294967296 | bytes 14680064 | tf_op jit(solution)/shard_map/dot_general | solution.py:14
  357.7 35.3 %all-gather.14.cloned.1.call-done = bf16[512,2048]{0,1:T(8,128)(2,1)} async-done(((bf16[128,2048]{0,1:T(8,128)(2,1)}), bf16[512,2048]{0,1:T(8,128)(2,1)}) %all-gather.14.cloned.1.call-update) | async-done | bytes 2097168 | tf_op jit(solution)/shard_map/all_gather | solution.py:65
  393.0 11.7 %convolution_add_fusion = f32[512,2048]{1,0:T(8,128)} fusion(f32[512,2048]{1,0:T(8,128)} %fusion.3, bf16[512,2048]{0,1:T(8,128)(2,1)} %all-gather.14.cloned.1.call-done, bf16[2048,2048]{0,1:T(8,128)(2,1)} %get-tuple-element.14), kind=kOutput, calls=%fused_computation.12 | convolution fusion | flops 4296015872 | bytes 18874368 | tf_op jit(solution)/shard_map/dot_general | solution.py:14
  405.1 34.0 %all-gather.8.cloned.1.call-done = bf16[512,2048]{0,1:T(8,128)(2,1)} async-done(((bf16[128,2048]{0,1:T(8,128)(2,1)}), bf16[512,2048]{0,1:T(8,128)(2,1)}) %all-gather.8.cloned.1.call-update) | async-done | bytes 2097168 | tf_op jit(solution)/shard_map/all_gather | solution.py:43
  439.1 10.5 %fusion.2 = f32[512,2048]{1,0:T(8,128)} fusion(bf16[512,2048]{0,1:T(8,128)(2,1)} %all-gather.8.cloned.1.call-done, bf16[2048,2048]{1,0:T(8,128)(2,1)} %bitcast_multiply_fusion.2), kind=kOutput, calls=%fused_computation.19 | convolution fusion | flops 4294967296 | bytes 14680064 | tf_op jit(solution)/shard_map/dot_general | solution.py:46
  449.6 8.5 %fusion = bf16[2048,2048]{0,1:T(8,128)(2,1)} fusion(bf16[512,2048]{0,1:T(8,128)(2,1)} %all-gather.12.cloned.1.call-done, bf16[512,2048]{1,0:T(8,128)(2,1)S(1)} %copy-done.4, bf16[2048,8]{0,1:T(8,128)(2,1)S(1)} %bitcast.51), kind=kOutput, calls=%fused_computation.4 | convolution fusion | flops 4307550208 | bytes 12615680 | tf_op jit(solution)/shard_map/dot_general | solution.py:20
  458.1 12.0 %copy.16 = bf16[2048,2048]{1,0:T(8,128)(2,1)} copy(bf16[2048,2048]{0,1:T(8,128)(2,1)} %fusion) | data formatting | bytes 16777216
  470.1 8.3 %fusion.1 = bf16[2048,2048]{0,1:T(8,128)(2,1)} fusion(bf16[512,2048]{0,1:T(8,128)(2,1)S(1)} %copy-done.1, bf16[512,2048]{1,0:T(8,128)(2,1)} %all-gather.6.cloned.1.call-done, bf16[2048,8]{0,1:T(8,128)(2,1)S(1)} %bitcast.52), kind=kOutput, calls=%fused_computation.5 | convolution fusion | flops 4307550208 | bytes 12615680 | tf_op jit(solution)/shard_map/dot_general | solution.py:20
  478.4 12.4 %copy.17 = bf16[2048,2048]{1,0:T(8,128)(2,1)} copy(bf16[2048,2048]{0,1:T(8,128)(2,1)} %fusion.1) | data formatting | bytes 16777216
  490.8 8.4 %multiply_convert_fusion = bf16[2048,2048]{1,0:T(8,128)(2,1)} fusion(bf16[512,2048]{0,1:T(8,128)(2,1)} %all-gather.8.cloned.1.call-done, bf16[512,2048]{1,0:T(8,128)(2,1)S(1)} %copy-done.3, bf16[2048,8]{0,1:T(8,128)(2,1)S(1)} %bitcast.49), kind=kOutput, calls=%fused_computation.6 | convolution fusion | flops 4307550208 | bytes 12615680 | tf_op jit(solution)/shard_map/dot_general | solution.py:20
  501.0 45.4 %reduce-scatter.7.cloned.1.call-done = f32[64,2048]{1,0:T(8,128)} async-done(((f32[512,2048]{1,0:T(8,128)}), f32[64,2048]{1,0:T(8,128)}) %reduce-scatter.7.cloned.1.call-update) | async-done | bytes 524304 | tf_op jit(solution)/shard_map/reduce_scatter | solution.py:45
  (38 shorter events, 8.7 us)
Async XLA Ops:
  7.2 33.2 %all-gather.10.cloned.1.call-start = ((), (), s32[]{:S(2)}) async-start(), calls=%async_computation.8 | async-start | bytes 2359296 | tf_op jit(solution)/shard_map/all_gather | solution.py:51
  7.9 82.0 %all-gather.6.cloned.1.call-start = ((), (), s32[]{:S(2)}) async-start(), calls=%async_computation.4 | async-start | bytes 2359296 | tf_op jit(solution)/shard_map/all_gather | solution.py:32
  8.7 140.6 %reduce-scatter.9.cloned.1.call-start = ((), (), s32[]{:S(2)}) async-start(), calls=%async_computation.9 | async-start | bytes 5242880 | tf_op jit(solution)/shard_map/reduce_scatter | solution.py:56
  50.9 0.7 copy-start.2
  50.9 245.6 %reduce-scatter.5.cloned.1.call-start = ((), (), s32[]{:S(2)}) async-start(), calls=%async_computation.5 | async-start | bytes 10485760 | tf_op jit(solution)/shard_map/reduce_scatter | solution.py:36
  89.9 7.8 %copy-start = (bf16[2048,2048]{0,1:T(8,128)(2,1)S(1)}, bf16[2048,2048]{0,1:T(8,128)(2,1)}, u32[]{:S(2)}) copy-start(bf16[2048,2048]{0,1:T(8,128)(2,1)} %get-tuple-element.13) | copy-start | bytes 25165828
  89.9 7.8 %copy-start.4 = (bf16[512,2048]{1,0:T(8,128)(2,1)S(1)}, bf16[512,2048]{1,0:T(8,128)(2,1)}, u32[]{:S(2)}) copy-start(bf16[512,2048]{1,0:T(8,128)(2,1)} %all-gather.6.cloned.1.call-done) | copy-start | bytes 6291460
  106.8 240.4 %all-gather.12.cloned.1.call-start = ((), (), s32[]{:S(2)}) async-start(), calls=%async_computation.10 | async-start | bytes 2621440 | tf_op jit(solution)/shard_map/all_gather | solution.py:64
  300.1 92.9 %all-gather.14.cloned.1.call-start = ((), (), s32[]{:S(2)}) async-start(), calls=%async_computation.11 | async-start | bytes 2621440 | tf_op jit(solution)/shard_map/all_gather | solution.py:65
  300.7 138.4 %all-gather.8.cloned.1.call-start = ((), (), s32[]{:S(2)}) async-start(), calls=%async_computation.6 | async-start | bytes 2621440 | tf_op jit(solution)/shard_map/all_gather | solution.py:43
  301.4 197.7 %reduce-scatter.11.cloned.1.call-start = ((), (), s32[]{:S(2)}) async-start(), calls=%async_computation.12 | async-start | bytes 4718592 | tf_op jit(solution)/shard_map/reduce_scatter | solution.py:70
  404.8 141.6 %reduce-scatter.7.cloned.1.call-start = ((), (), s32[]{:S(2)}) async-start(), calls=%async_computation.7 | async-start | bytes 4718592 | tf_op jit(solution)/shard_map/reduce_scatter | solution.py:45
  458.1 12.0 %copy-start.1 = (bf16[512,2048]{0,1:T(8,128)(2,1)S(1)}, bf16[512,2048]{0,1:T(8,128)(2,1)}, u32[]{:S(2)}) copy-start(bf16[512,2048]{0,1:T(8,128)(2,1)} %all-gather.14.cloned.1.call-done) | copy-start | bytes 6291460
  478.4 12.4 %copy-start.3 = (bf16[512,2048]{1,0:T(8,128)(2,1)S(1)}, bf16[512,2048]{1,0:T(8,128)(2,1)}, u32[]{:S(2)}) copy-start(bf16[512,2048]{1,0:T(8,128)(2,1)} %all-gather.10.cloned.1.call-done) | copy-start | bytes 6291460
Sparse Core Ops, SparseCore 0:
  9.9 30.4 all-gather.9
  42.3 27.7 all-gather.5
  72.4 76.7 reduce-scatter.8
  151.4 145.1 reduce-scatter.4
  300.2 46.8 all-gather.11
  348.6 44.4 all-gather.13
  394.6 44.4 all-gather.7
  442.4 49.3 reduce-scatter.10
  495.2 51.1 reduce-scatter.6
where the time goes:
time: 556 us; the launch traced here: 555 us
  waiting for transfers between devices  376 us (68%)
  matrix products  81.1 us (15%)
  local copies, waits for them, and re-layouts  49.6 us (9%)
  other arithmetic  33 us (6%)
  between operations  13.9 us (2%)
    reduce_scatter x1, waiting for transfers between devices, local(): lax.psum_scatter(jnp.concatenate([gate_part, up_part], axis=1), 'row', sc...  147 us
    unnamed x14, local copies, waits for them, and re-layouts  49.3 us
    all_gather x1, waiting for transfers between devices, local(): lax.all_gather(gate_grad, 'row', axis=0, tiled=True)  45.4 us
    reduce_scatter x1, waiting for transfers between devices, local(): lax.psum_scatter(jnp.dot(row_block, down_masked, preferred_element_type=j...  45.4 us
    reduce_scatter x1, waiting for transfers between devices, local(): lax.psum_scatter(transposed_right(row_block, down_masked), 'row', scatter...  42.4 us
    all_gather x1, waiting for transfers between devices, local(): lax.all_gather(up_grad, 'row', axis=0, tiled=True)  35.3 us
    all_gather x1, waiting for transfers between devices, local(): hidden_full = lax.all_gather(hidden_share, 'row', axis=0, tiled=True)  34 us
    dot_general x3, matrix products, transposed_right(): lax.dot_general(left, right, (((1,), (1,)), ((), ())), preferred_element_...  32.8 us
  transfers between devices with their start and end apart: 9, of which 7 were waited for; matrix products, arithmetic and copies ran while one was open for 28% of the time, Pallas kernels for 0%

commit v1 on v0

--- a/solution.py
+++ b/solution.py
@@ -40,7 +40,9 @@
     up = joined[:, hidden_width:]
     sigmoid_gate = jax.nn.sigmoid(gate)
     hidden_share = (gate * sigmoid_gate * up).astype(jnp.bfloat16)
-    hidden_full = lax.all_gather(hidden_share, "row", axis=0, tiled=True)
+    even = lax.axis_size("row")
+    w_next = jnp.concatenate([hidden_share] * even, 0)
+    hidden_full = lax.all_to_all(w_next, axis_name="row", split_axis=0, concat_axis=0, tiled=True)
     row_block = hidden_full
     output = lax.psum_scatter(
         jnp.dot(row_block, down_masked, preferred_element_type=jnp.float32),

time: 556 us -> 533 us (0.959)
  waiting for transfers between devices: 376 us -> 297 us
  blocking collectives: 0 us -> 50.9 us
    all_to_all x0 -> x1, blocking collectives: none -> 50.9 us  [local(): lax.all_to_all(w_next, axis_name='row', split_axis=0, concat_axis=0, tile...]
    reduce_scatter x1, waiting for transfers between devices: 45.4 us -> 0.01 us  [local(): lax.psum_scatter(jnp.dot(row_block, down_masked, preferred_element_type=j...]
    all_gather x1 -> x0, waiting for transfers between devices: 34 us -> none  [local(): hidden_full = lax.all_gather(hidden_share, 'row', axis=0, tiled=True)]
    unnamed x14 -> x16, local copies, waits for them, and re-layouts: 49.3 us -> 51.5 us
  transfers between devices with their start and end apart: 9 -> 8, of which waited for: 7 -> 5; matrix products, arithmetic and copies ran while one was open for 28% -> 28% of each run, Pallas kernels for 0% -> 0%
where the time goes in v1:
time: 533 us; the launch traced here: 531 us
  waiting for transfers between devices  297 us (56%)
  matrix products  80.8 us (15%)
  local copies, waits for them, and re-layouts  54.5 us (10%)
  blocking collectives  50.9 us (10%)
  other arithmetic  33.2 us (6%)
  between operations  14.2 us (3%)
    reduce_scatter x1, waiting for transfers between devices, local(): lax.psum_scatter(jnp.concatenate([gate_part, up_part], axis=1), 'row', sc...  147 us
    unnamed x16, local copies, waits for them, and re-layouts  51.5 us
    all_to_all x1, blocking collectives, local(): lax.all_to_all(w_next, axis_name='row', split_axis=0, concat_axis=0, tile...  50.9 us
    all_gather x1, waiting for transfers between devices, local(): lax.all_gather(gate_grad, 'row', axis=0, tiled=True)  46.2 us
    reduce_scatter x1, waiting for transfers between devices, local(): lax.psum_scatter(transposed_right(row_block, down_masked), 'row', scatter...  42.4 us
    all_gather x1, waiting for transfers between devices, local(): lax.all_gather(up_grad, 'row', axis=0, tiled=True)  35.3 us
    dot_general x3, matrix products, transposed_right(): lax.dot_general(left, right, (((1,), (1,)), ((), ())), preferred_element_...  32.8 us
    dot_general x3, matrix products, transposed_left(): lax.dot_general(left, right, (((0,), (0,)), ((), ())), preferred_element_...  25 us
  transfers between devices with their start and end apart: 8, of which 5 were waited for; matrix products, arithmetic and copies ran while one was open for 28% of the time, Pallas kernels for 0%

profile of v1, /device:TPU:0, one launch (start us, length us, event | category | flops | bytes accessed | tf_op | source)
XLA Modules:
  0.0 531.1 jit_solution(96348326615821059)
XLA Ops:
  9.6 7.3 %bitcast_multiply_fusion.2 = bf16[2048,2048]{1,0:T(8,128)(2,1)} fusion(bf16[2048,2048]{1,0:T(8,128)(2,1)} %param.10, bf16[2048,8]{0,1:T(8,128)(2,1)S(1)} %bitcast.56), kind=kLoop, calls=%fused_computation.7 | loop fusion | flops 4194304 | bytes 16809984 | tf_op jit(solution)/shard_map/mul | solution.py:30
  16.9 23.5 %all-gather.7.cloned.1.call-done = bf16[512,2048]{1,0:T(8,128)(2,1)} async-done(((bf16[64,2048]{1,0:T(8,128)(2,1)}), bf16[512,2048]{1,0:T(8,128)(2,1)}) %all-gather.7.cloned.1.call-update) | async-done | bytes 2097168 | tf_op jit(solution)/shard_map/all_gather | solution.py:53
  40.4 10.5 %convolution_bitcast_fusion = f32[512,2048]{0,1:T(8,128)} fusion(bf16[2048,2048]{1,0:T(8,128)(2,1)} %bitcast_multiply_fusion.2, bf16[512,2048]{1,0:T(8,128)(2,1)} %all-gather.7.cloned.1.call-done), kind=kOutput, calls=%fused_computation.9 | convolution fusion | flops 4294967296 | bytes 14680064 | tf_op jit(solution)/shard_map/dot_general | solution.py:14
  51.7 12.2 %copy.26 = bf16[2048,2048]{0,1:T(8,128)(2,1)} copy(bf16[2048,2048]{1,0:T(8,128)(2,1)} %param.8) | data formatting | bytes 16777216 | tf_op args[1]
  63.9 12.2 %copy.27 = bf16[2048,2048]{0,1:T(8,128)(2,1)} copy(bf16[2048,2048]{1,0:T(8,128)(2,1)} %param.9) | data formatting | bytes 16777216 | tf_op args[2]
  76.2 13.7 %bitcast_multiply_fusion.1 = (bf16[2048,2048]{0,1:T(8,128)(2,1)}, bf16[2048,2048]{0,1:T(8,128)(2,1)}) fusion(bf16[2048,2048]{0,1:T(8,128)(2,1)} %copy.26, bf16[2048,8]{0,1:T(8,128)(2,1)S(1)} %bitcast.58, bf16[2048,2048]{0,1:T(8,128)(2,1)} %copy.27), kind=kLoop, calls=%fused_computation.3 | loop fusion | flops 8388608 | bytes 33587200 | tf_op jit(solution)/shard_map/mul | solution.py:28
  89.9 7.8 %convolution_bitcast_fusion.1 = f32[512,2048]{0,1:T(8,128)S(1)} fusion(bf16[2048,2048]{0,1:T(8,128)(2,1)} %get-tuple-element.24, bf16[512,2048]{1,0:T(8,128)(2,1)} %all-gather.5.cloned.1.call-done), kind=kOutput, calls=%fused_computation.10 | convolution fusion | flops 4294967296 | bytes 14680064 | tf_op jit(solution)/shard_map/dot_general | solution.py:35
  97.7 4.8 convolution_bitcast_fusion.2
  102.5 4.2 pad_maximum_fusion
  106.8 42.4 %reduce-scatter.9.cloned.1.call-done = f32[128,2048]{0,1:T(8,128)} async-done(((f32[512,2048]{0,1:T(8,128)}), f32[128,2048]{0,1:T(8,128)}) %reduce-scatter.9.cloned.1.call-update) | async-done | bytes 1048592 | tf_op jit(solution)/shard_map/reduce_scatter | solution.py:58
  149.2 147.4 %reduce-scatter.5.cloned.1.call-done = f32[128,4096]{0,1:T(8,128)} async-done(((f32[512,4096]{0,1:T(8,128)}), f32[128,4096]{0,1:T(8,128)}) %reduce-scatter.5.cloned.1.call-update) | async-done | bytes 2097168 | tf_op jit(solution)/shard_map/reduce_scatter | solution.py:36
  296.6 3.4 multiply_convert_fusion.1
  300.9 46.2 %all-gather.9.cloned.1.call-done = bf16[512,2048]{0,1:T(8,128)(2,1)} async-done(((bf16[128,2048]{0,1:T(8,128)(2,1)}), bf16[512,2048]{0,1:T(8,128)(2,1)}) %all-gather.9.cloned.1.call-update) | async-done | bytes 2097168 | tf_op jit(solution)/shard_map/all_gather | solution.py:66
  347.1 10.6 %fusion.3 = f32[512,2048]{1,0:T(8,128)} fusion(bf16[512,2048]{0,1:T(8,128)(2,1)} %all-gather.9.cloned.1.call-done, bf16[2048,2048]{0,1:T(8,128)(2,1)} %get-tuple-element.23), kind=kOutput, calls=%fused_computation.22 | convolution fusion | flops 4294967296 | bytes 14680064 | tf_op jit(solution)/shard_map/dot_general | solution.py:14
  357.6 35.3 %all-gather.11.cloned.1.call-done = bf16[512,2048]{0,1:T(8,128)(2,1)} async-done(((bf16[128,2048]{0,1:T(8,128)(2,1)}), bf16[512,2048]{0,1:T(8,128)(2,1)}) %all-gather.11.cloned.1.call-update) | async-done | bytes 2097168 | tf_op jit(solution)/shard_map/all_gather | solution.py:67
  393.0 11.7 %convolution_add_fusion = f32[512,2048]{1,0:T(8,128)} fusion(f32[512,2048]{1,0:T(8,128)} %fusion.3, bf16[512,2048]{0,1:T(8,128)(2,1)} %all-gather.11.cloned.1.call-done, bf16[2048,2048]{0,1:T(8,128)(2,1)} %get-tuple-element.24), kind=kOutput, calls=%fused_computation.12 | convolution fusion | flops 4296015872 | bytes 18874368 | tf_op jit(solution)/shard_map/dot_general | solution.py:14
  405.0 50.9 %all_to_all.12 = bf16[4,128,2048]{1,2,0:T(8,128)(2,1)S(1)} all-to-all(bf16[4,128,2048]{1,2,0:T(8,128)(2,1)S(1)} %copy_bitcast_fusion), channel_id=1, replica_groups=mesh['row'=4,'col'=8] {'row'}, dimensions={0} | all-to-all | bytes 4194304 | tf_op jit(solution)/shard_map/all_to_all | solution.py:45
  456.0 2.7 copy.29
  458.7 10.5 %fusion.2 = f32[512,2048]{1,0:T(8,128)} fusion(bf16[512,2048]{1,0:T(8,128)(2,1)} %bitcast.54, bf16[2048,2048]{1,0:T(8,128)(2,1)} %bitcast_multiply_fusion.2), kind=kOutput, calls=%fused_computation.21 | convolution fusion | flops 4294967296 | bytes 14680064 | tf_op jit(solution)/shard_map/dot_general | solution.py:48
  470.7 8.3 %fusion = bf16[2048,2048]{0,1:T(8,128)(2,1)} fusion(bf16[512,2048]{0,1:T(8,128)(2,1)} %all-gather.9.cloned.1.call-done, bf16[512,2048]{1,0:T(8,128)(2,1)S(1)} %copy-done.5, bf16[2048,8]{0,1:T(8,128)(2,1)S(1)} %bitcast.59), kind=kOutput, calls=%fused_computation.4 | convolution fusion | flops 4307550208 | bytes 12615680 | tf_op jit(solution)/shard_map/dot_general | solution.py:20
  479.0 12.5 %copy.31 = bf16[2048,2048]{1,0:T(8,128)(2,1)} copy(bf16[2048,2048]{0,1:T(8,128)(2,1)} %fusion) | data formatting | bytes 16777216
  491.6 8.3 %fusion.1 = bf16[2048,2048]{0,1:T(8,128)(2,1)} fusion(bf16[512,2048]{0,1:T(8,128)(2,1)S(1)} %copy-done.1, bf16[512,2048]{1,0:T(8,128)(2,1)} %all-gather.5.cloned.1.call-done, bf16[2048,8]{0,1:T(8,128)(2,1)S(1)} %bitcast.60), kind=kOutput, calls=%fused_computation.5 | convolution fusion | flops 4307550208 | bytes 12615680 | tf_op jit(solution)/shard_map/dot_general | solution.py:20
  499.9 12.5 %copy.32 = bf16[2048,2048]{1,0:T(8,128)(2,1)} copy(bf16[2048,2048]{0,1:T(8,128)(2,1)} %fusion.1) | data formatting | bytes 16777216
  512.3 8.4 %multiply_convert_fusion = bf16[2048,2048]{1,0:T(8,128)(2,1)} fusion(bf16[512,2048]{1,0:T(8,128)(2,1)S(1)} %bitcast.55, bf16[512,2048]{1,0:T(8,128)(2,1)} %all-gather.7.cloned.1.call-done, bf16[2048,8]{0,1:T(8,128)(2,1)S(1)} %bitcast.57), kind=kOutput, calls=%fused_computation.6 | convolution fusion | flops 4307550208 | bytes 12615680 | tf_op jit(solution)/shard_map/dot_general | solution.py:20
  (40 shorter events, 9.6 us)
Async XLA Ops:
  7.2 33.2 %all-gather.7.cloned.1.call-start = ((), (), s32[]{:S(2)}) async-start(), calls=%async_computation.8 | async-start | bytes 2359296 | tf_op jit(solution)/shard_map/all_gather | solution.py:53
  7.9 82.0 %all-gather.5.cloned.1.call-start = ((), (), s32[]{:S(2)}) async-start(), calls=%async_computation.5 | async-start | bytes 2359296 | tf_op jit(solution)/shard_map/all_gather | solution.py:32
  8.7 140.6 %reduce-scatter.9.cloned.1.call-start = ((), (), s32[]{:S(2)}) async-start(), calls=%async_computation.9 | async-start | bytes 5242880 | tf_op jit(solution)/shard_map/reduce_scatter | solution.py:58
  50.9 0.7 copy-start.3
  50.9 245.7 %reduce-scatter.5.cloned.1.call-start = ((), (), s32[]{:S(2)}) async-start(), calls=%async_computation.6 | async-start | bytes 10485760 | tf_op jit(solution)/shard_map/reduce_scatter | solution.py:36
  89.9 7.8 %copy-start = (bf16[2048,2048]{0,1:T(8,128)(2,1)S(1)}, bf16[2048,2048]{0,1:T(8,128)(2,1)}, u32[]{:S(2)}) copy-start(bf16[2048,2048]{0,1:T(8,128)(2,1)} %get-tuple-element.23) | copy-start | bytes 25165828
  89.9 7.8 %copy-start.4 = (bf16[512,2048]{1,0:T(8,128)(2,1)S(1)}, bf16[512,2048]{1,0:T(8,128)(2,1)}, u32[]{:S(2)}) copy-start(bf16[512,2048]{1,0:T(8,128)(2,1)} %all-gather.5.cloned.1.call-done) | copy-start | bytes 6291460
  106.7 240.3 %all-gather.9.cloned.1.call-start = ((), (), s32[]{:S(2)}) async-start(), calls=%async_computation.10 | async-start | bytes 2621440 | tf_op jit(solution)/shard_map/all_gather | solution.py:66
  300.1 92.9 %all-gather.11.cloned.1.call-start = ((), (), s32[]{:S(2)}) async-start(), calls=%async_computation.11 | async-start | bytes 2621440 | tf_op jit(solution)/shard_map/all_gather | solution.py:67
  300.6 220.1 %reduce-scatter.11.cloned.1.call-start = ((), (), s32[]{:S(2)}) async-start(), calls=%async_computation.12 | async-start | bytes 4718592 | tf_op jit(solution)/shard_map/reduce_scatter | solution.py:72
  404.7 117.8 %reduce-scatter.7.cloned.1.call-start = ((), (), s32[]{:S(2)}) async-start(), calls=%async_computation.7 | async-start | bytes 4718592 | tf_op jit(solution)/shard_map/reduce_scatter | solution.py:47
  469.1 1.6 copy-start.5
  479.0 12.5 %copy-start.1 = (bf16[512,2048]{0,1:T(8,128)(2,1)S(1)}, bf16[512,2048]{0,1:T(8,128)(2,1)}, u32[]{:S(2)}) copy-start(bf16[512,2048]{0,1:T(8,128)(2,1)} %all-gather.11.cloned.1.call-done) | copy-start | bytes 6291460
  499.9 12.5 %copy-start.2 = (bf16[4,128,2048]{2,1,0:T(8,128)(2,1)S(1)}, bf16[4,128,2048]{2,1,0:T(8,128)(2,1)}, u32[]{:S(2)}) copy-start(bf16[4,128,2048]{2,1,0:T(8,128)(2,1)} %copy.29) | copy-start | bytes 6291460
Sparse Core Ops, SparseCore 0:
  9.9 30.4 all-gather.6
  42.3 27.7 all-gather.4
  72.4 76.7 reduce-scatter.8
  151.4 145.1 reduce-scatter.4
  300.2 46.8 all-gather.8
  348.5 44.4 all-gather.10
  404.8 49.3 reduce-scatter.10
  469.3 50.2 reduce-scatter.6
